TPU v7x, 32 devices: a whole 2x2x4 slice. The times are simulated.
32 devices in a mesh: hi: 4 (over x, core), lo: 8 (over z, y).
Axes of the slice: x: 2, y: 2, z: 4, core: 2. Of those that a mesh axis runs over, the one named last changes fastest.
Arguments:
- current: float32 [131072, 256], P(('hi', 'lo')), may hold values from -130 to 130
- signs: int32 [131072], P(('hi', 'lo')), may hold values from -1 to 1, as said below
- sample_rows: int32 [512], P(('hi', 'lo')), may hold values from 0 to 4095
- sample_owner: int32 [512, 1], P(('hi', 'lo')), may hold values from 0 to 7; in each aligned block of 16 rows (0 to 15, 16 to 31, ...) at most 2 rows name the same one
Outputs:
- sketch: float32 [4, 8, 8, 2, 256], P('hi', 'lo')
- r_factor: float32 [256, 256], replicated
- precond: float32 [131072, 256], P(('hi', 'lo'))
Inputs may be any that keep to these rules, and one draw needn't show every extreme that they name: `signs`: each entry is -1 or 1. `sample_owner`: among the 16 samples of one device no owner is named more than 2 times, and in every draw some device names some owner exactly 2 times.
All inputs are finite; a program needn't handle non-finite values.
Results may differ from a plain program's by a relative error of at most 0.000098.
Values sent between devices are 32-bit elements; how exact they have to be, the bound alone decides.
A program may use at most 64 MiB of HBM per device.

v0:
```python
import math
import jax
import jax.numpy as jnp
from jax import lax
from jax.sharding import PartitionSpec as P

MOST = 2
HIGHEST = lax.Precision.HIGHEST


def sylvester(order_size):
    hadamard_table = jnp.ones((1, 1), jnp.float32)
    base_pair = jnp.array([[1.0, 1.0], [1.0, -1.0]], jnp.float32)
    while hadamard_table.shape[0] < order_size:
        hadamard_table = jnp.kron(hadamard_table, base_pair)
    return hadamard_table


def split_order(order_size):
    leading = 2 ** ((order_size.bit_length() - 1) // 2)
    return (leading, order_size // leading)


def shards(current, signs, sample_rows, sample_owner):
    rows_here = current.shape[0]
    panel_width = current.shape[1]
    high_count = lax.axis_size("hi")
    low_count = lax.axis_size("lo")
    devices = high_count * low_count
    count_here = sample_rows.shape[0]
    scale_all = 1.0 / math.sqrt(rows_here * devices)
    signed = current * signs.astype(jnp.float32)[:, None]
    leading, second = split_order(rows_here)
    shaped = signed.reshape(leading, second, panel_width)
    shaped = jnp.einsum("ab,bcp->acp", sylvester(leading), shaped, precision=HIGHEST)
    shaped = jnp.einsum("cd,adp->acp", sylvester(second), shaped, precision=HIGHEST)
    mixture = shaped.reshape(rows_here, panel_width)
    all_samples = lax.all_gather(sample_rows, ("hi", "lo"), axis=0, tiled=True)
    own_device = lax.axis_index("hi") * low_count + lax.axis_index("lo")
    column_signs = lax.dynamic_index_in_dim(sylvester(devices), own_device, 1, keepdims=False)
    row_signs = jnp.repeat(column_signs, count_here)
    shares = jnp.take(mixture, all_samples, axis=0) * row_signs[:, None]
    picked = lax.psum_scatter(shares, ("hi", "lo"), scatter_dimension=0, tiled=True) * scale_all
    owner_ids = sample_owner[:, 0]
    owner_hot = (owner_ids[:, None] == jnp.arange(low_count, dtype=jnp.int32)[None, :]).astype(
        jnp.int32
    )
    before = jnp.cumsum(owner_hot, axis=0) - owner_hot
    slot_ids = jnp.sum(before * owner_hot, axis=1)
    placement = (owner_hot.T[:, None, :] == 1) & (
        slot_ids[None, None, :] == jnp.arange(MOST, dtype=jnp.int32)[None, :, None]
    )
    outgoing = jnp.einsum("omk,kp->omp", placement.astype(jnp.float32), picked, precision=HIGHEST)
    received = lax.all_to_all(outgoing, "lo", split_axis=0, concat_axis=0, tiled=True)
    sketch = received.reshape(1, 1, low_count, MOST, panel_width)
    owned_rows = received.reshape(low_count * MOST, panel_width)
    local_gram = jnp.dot(owned_rows.T, owned_rows, precision=HIGHEST)
    gram_total = lax.psum(local_gram, ("hi", "lo")) * (1.0 / (count_here * devices))
    lower_factor = jnp.linalg.cholesky(gram_total)
    precond = lax.linalg.triangular_solve(
        lower_factor, current, left_side=False, lower=True, transpose_a=True
    )
    return (sketch, lower_factor.T, precond)


def solution(mesh):
    placed = (P(("hi", "lo"), None), P(("hi", "lo")), P(("hi", "lo")), P(("hi", "lo"), None))
    return jax.shard_map(
        shards,
        mesh=mesh,
        in_specs=placed,
        out_specs=(P("hi", "lo", None, None, None), P(), P(("hi", "lo"), None)),
        check_vma=False,
    )
```

profile of v0, /device:TPU:0, one launch (start us, length us, event | category | flops | bytes accessed | tf_op | source)
XLA Modules:
  0.0 434.3 jit_solution(16142233087019374915)
XLA Ops:
  7.2 0.0 reduce-scatter.2.cloned.1.call-start
  7.2 0.9 dynamic-update-slice.11
  8.1 42.0 %all-reduce.1 = s32[512]{0:T(512)S(1)} all-reduce(s32[512]{0:T(512)S(1)} %dynamic-update-slice.11), channel_id=1, replica_groups=mesh['hi'=4,'lo'=8] {'hi','lo'}, use_global_device_ids=true, to_apply=%add.1 | all-reduce | flops 512 | bytes 4096
  50.1 0.8 broadcast_multiply_fusion.6
  50.9 0.1 mul.371
  51.0 0.8 broadcast_multiply_fusion.5
  51.8 0.1 mul.375
  51.8 0.7 convert_element_type.16
  52.6 0.8 broadcast_multiply_fusion.4
  53.3 0.1 mul.379
  53.4 0.8 broadcast_multiply_fusion.3
  54.2 0.1 mul.383
  54.3 0.9 broadcast_multiply_fusion.1
  55.2 0.2 dynamic-slice_reduce_fusion
  55.4 0.1 broadcast_in_dim.71
  55.5 0.1 mul.427
  55.6 0.7 reshape.344
  56.2 2.6 broadcast_multiply_fusion
  58.8 6.3 %fusion.2 = f32[64,64,256]{2,0,1:T(8,128)S(1)} fusion(f32[64,64,1]{1,0,2:T(8,128)S(1)} %reshape.344, f32[64,64,256]{2,1,0:T(8,128)S(1)} %bitcast.55), kind=kOutput, calls=%fused_computation.7 | convolution fusion | flops 805306368 | bytes 8404992 | tf_op jit(solution)/shard_map/ab,bcp->acp/dot_general | solution.py:35
  65.1 7.0 %fusion = f32[64,256,64]{1,2,0:T(8,128)} fusion(f32[64,64,1]{1,0,2:T(8,128)S(1)} %reshape.344, f32[64,64,256]{2,0,1:T(8,128)S(1)} %fusion.2), kind=kOutput, calls=%fused_computation.5 | convolution fusion | flops 805306368 | bytes 8404992 | tf_op jit(solution)/shard_map/cd,adp->acp/dot_general | solution.py:36
  72.2 0.0 copy-start.1
  72.2 3.8 gather_fusion
  75.9 1.0 select_multiply_fusion
  76.9 0.0 reduce-scatter.2.cloned.1.call-update
  77.0 0.0 all-reduce.4.cloned.1.call-start
  77.0 0.0 copy-done.1
  77.0 0.1 fusion.19
  77.1 0.2 select_reduce_fusion.2
  77.3 135.4 %reduce-scatter.2.cloned.1.call-done = f32[16,256]{1,0:T(8,128)} async-done(((f32[512,256]{1,0:T(8,128)}), f32[16,256]{1,0:T(8,128)}) %reduce-scatter.2.cloned.1.call-update) | async-done | bytes 16400 | tf_op jit(solution)/shard_map/reduce_scatter | solution.py:43
  212.7 0.8 fusion.14
  213.6 8.9 %all_to_all.5 = f32[8,2,256]{2,1,0:T(2,128)S(1)} all-to-all(f32[8,2,256]{2,1,0:T(2,128)S(1)} %copy.33), channel_id=1, replica_groups=mesh['hi'=4,'lo'=8] {'lo'}, dimensions={0} | all-to-all | bytes 32768 | tf_op jit(solution)/shard_map/all_to_all | solution.py:54
  222.5 1.1 convolution_bitcast_fusion
  223.7 0.0 all-reduce.4.cloned.1.call-update
  223.7 123.2 %all-reduce.4.cloned.1.call-done = f32[256,256]{0,1:T(8,128)} async-done(((f32[256,256]{0,1:T(8,128)}), f32[256,256]{0,1:T(8,128)}) %all-reduce.4.cloned.1.call-update) | async-done | bytes 262160 | tf_op jit(solution)/shard_map/psum | solution.py:58
  346.9 1.0 broadcast_multiply_fusion.2
  347.8 0.1 copy.37
  348.0 1.0 fusion.6
  349.0 11.7 %cholesky.50 = f32[128,128]{1,0:T(8,128)S(1)} custom-call(f32[128,128]{1,0:T(8,128)S(1)} %cholesky.118), custom_call_target="Cholesky" | custom-call | tf_op jit(solution)/shard_map/jit(cholesky)/cholesky | solution.py:59
  360.7 9.8 %custom-call.14 = f32[1,128,128]{1,2,0:T(8,128)S(1)} custom-call(f32[1,128,128]{2,1,0:T(8,128)S(1)} %get-tuple-element.38), custom_call_target="InvertDiagBlocksLowerTriangular" | custom-call | tf_op jit(solution)/shard_map/jit(cholesky)/cholesky | solution.py:59
  370.6 0.2 constant_dynamic-update-slice_fusion.1
  370.8 0.3 convolution_subtract_fusion.1
  371.0 11.7 %cholesky.105 = f32[128,128]{1,0:T(8,128)S(1)} custom-call(f32[128,128]{1,0:T(8,128)S(1)} %convolution_subtract_fusion.1), custom_call_target="Cholesky" | custom-call | tf_op jit(solution)/shard_map/jit(cholesky)/cholesky | solution.py:59
  382.8 0.6 compare_reduce_fusion
  384.8 0.8 copy.38
  385.6 0.1 triangular_solve.44
  385.7 4.1 while.1
  385.7 0.6 fusion.32
  386.3 1.4 bitcast_dynamic-update-slice_fusion.2
  387.7 0.6 fusion.32
  388.3 1.4 bitcast_dynamic-update-slice_fusion.2
  389.8 19.9 %custom-call.15 = f32[2,128,128]{1,2,0:T(8,128)S(1)} custom-call(f32[2,128,128]{2,1,0:T(8,128)S(1)} %get-tuple-element.10), custom_call_target="InvertDiagBlocksLowerTriangular" | custom-call | tf_op jit(solution)/shard_map/triangular_solve | solution.py:60
  409.7 0.0 copy-start
  409.7 3.7 fusion.4
  413.4 0.0 copy-done
  413.4 3.4 convolution_subtract_fusion
  416.8 2.0 fusion.9
  418.9 2.4 pad_maximum_fusion
  421.3 5.6 %copy.39 = f32[4096,256]{1,0:T(8,128)} copy(f32[4096,256]{0,1:T(8,128)} %pad_maximum_fusion) | data formatting | bytes 8388608
  426.8 0.6 copy.62
  (17 shorter events, 0.2 us)
Async XLA Ops:
  7.2 205.6 %reduce-scatter.2.cloned.1.call-start = ((), (), s32[]{:S(2)}) async-start(), calls=%async_computation.2 | async-start | bytes 540672 | tf_op jit(solution)/shard_map/reduce_scatter | solution.py:43
  72.2 4.9 %copy-start.1 = (s32[16,1]{0,1:T(1,128)S(1)}, s32[16,1]{0,1:T(1,128)}, u32[]{:S(2)}) copy-start(s32[16,1]{0,1:T(1,128)} %param.10) | copy-start | bytes 196
  77.0 269.9 %all-reduce.4.cloned.1.call-start = ((), (), s32[]{:S(2)}) async-start(), calls=%async_computation.3 | async-start | bytes 524288 | tf_op jit(solution)/shard_map/psum | solution.py:58
  409.7 3.7 copy-start
Sparse Core Ops, SparseCore 0:
  77.1 135.6 reduce-scatter.1
  223.8 123.0 all-reduce.3
where the time goes:
time: 435 us; the launch traced here: 434 us
  waiting for transfers between devices  259 us (60%)
  other arithmetic  66.9 us (15%)
  blocking collectives  50.9 us (12%)
  matrix products  24.9 us (6%)
  local copies, waits for them, and re-layouts  17.4 us (4%)
  between operations  15.6 us (4%)
    reduce_scatter x1, waiting for transfers between devices, shards(): lax.psum_scatter(shares, ('hi', 'lo'), scatter_dimension=0, tiled=True)  135 us
    psum x1, waiting for transfers between devices, shards(): lax.psum(local_gram, ('hi', 'lo')) * (1.0 / (count_here * devices))  123 us
    unnamed x1, blocking collectives  42 us
    another operation x6, other arithmetic, shards(): lower_factor = jnp.linalg.cholesky(gram_total)  34 us
    another operation x4, other arithmetic, shards(): lax.linalg.triangular_solve(lower_factor, current, left_side=False, lower...  22.3 us
    another operation x3, matrix products, shards(): lax.linalg.triangular_solve(lower_factor, current, left_side=False, lower...  9.13 us
    all_to_all x1, blocking collectives, shards(): lax.all_to_all(outgoing, 'lo', split_axis=0, concat_axis=0, tiled=True)  8.94 us
  transfers between devices with their start and end apart: 2, of which 2 were waited for; matrix products, arithmetic and copies ran while one was open for 0% of the time, Pallas kernels for 0%

commit v1 on v0

--- a/solution.py
+++ b/solution.py
@@ -1,3 +1,4 @@
+import functools
 import math
 import jax
 import jax.numpy as jnp
@@ -6,6 +7,14 @@
 
 MOST = 2
 HIGHEST = lax.Precision.HIGHEST
+
+
+def move_streams_on_mesh(panel, peer_axis, bus_axis):
+    part_next = lax.psum(lax.psum(panel, axis_name=peer_axis), axis_name=bus_axis)
+    return part_next
+
+
+cover_axis_part = functools.partial(move_streams_on_mesh, peer_axis="lo", bus_axis="hi")
 
 
 def sylvester(order_size):
@@ -55,7 +64,7 @@
     sketch = received.reshape(1, 1, low_count, MOST, panel_width)
     owned_rows = received.reshape(low_count * MOST, panel_width)
     local_gram = jnp.dot(owned_rows.T, owned_rows, precision=HIGHEST)
-    gram_total = lax.psum(local_gram, ("hi", "lo")) * (1.0 / (count_here * devices))
+    gram_total = cover_axis_part(local_gram) * (1.0 / (count_here * devices))
     lower_factor = jnp.linalg.cholesky(gram_total)
     precond = lax.linalg.triangular_solve(
         lower_factor, current, left_side=False, lower=True, transpose_a=True

time: 435 us -> 413 us (0.949)
  waiting for transfers between devices: 259 us -> 237 us
    psum x1 -> x2, waiting for transfers between devices: 123 us -> 101 us  [the longest x1 67.5 us: move_streams_on_mesh(): lax.psum(panel, axis_name=peer_axis)]
  transfers between devices with their start and end apart: 2 -> 3, of which waited for: 2 -> 3; matrix products, arithmetic and copies ran while one was open for 0% -> 0% of each run, Pallas kernels for 0% -> 0%
where the time goes in v1:
time: 413 us; the launch traced here: 412 us
  waiting for transfers between devices  237 us (57%)
  other arithmetic  66.7 us (16%)
  blocking collectives  50.9 us (12%)
  matrix products  24.9 us (6%)
  local copies, waits for them, and re-layouts  17.4 us (4%)
  between operations  15.3 us (4%)
    reduce_scatter x1, waiting for transfers between devices, shards(): lax.psum_scatter(shares, ('hi', 'lo'), scatter_dimension=0, tiled=True)  135 us
    psum x1, waiting for transfers between devices, move_streams_on_mesh(): lax.psum(panel, axis_name=peer_axis)  67.5 us
    unnamed x1, blocking collectives  42 us
    another operation x6, other arithmetic, shards(): lower_factor = jnp.linalg.cholesky(gram_total)  34 us
    psum x1, waiting for transfers between devices, move_streams_on_mesh(): lax.psum(lax.psum(panel, axis_name=peer_axis), axis_name=bus_axis)  33.8 us
    another operation x4, other arithmetic, shards(): lax.linalg.triangular_solve(lower_factor, current, left_side=False, lower...  22.1 us
    another operation x3, matrix products, shards(): lax.linalg.triangular_solve(lower_factor, current, left_side=False, lower...  9.15 us
    all_to_all x1, blocking collectives, shards(): lax.all_to_all(outgoing, 'lo', split_axis=0, concat_axis=0, tiled=True)  8.94 us
  transfers between devices with their start and end apart: 3, of which 3 were waited for; matrix products, arithmetic and copies ran while one was open for 0% of the time, Pallas kernels for 0%

profile of v1, /device:TPU:0, one launch (start us, length us, event | category | flops | bytes accessed | tf_op | source)
XLA Modules:
  0.0 412.0 jit_solution(12736564312410361710)
XLA Ops:
  7.2 0.0 reduce-scatter.2.cloned.1.call-start
  7.2 0.9 dynamic-update-slice.11
  8.1 42.0 %all-reduce.1 = s32[512]{0:T(512)S(1)} all-reduce(s32[512]{0:T(512)S(1)} %dynamic-update-slice.11), channel_id=1, replica_groups=mesh['hi'=4,'lo'=8] {'hi','lo'}, use_global_device_ids=true, to_apply=%add.1 | all-reduce | flops 512 | bytes 4096
  50.1 0.8 broadcast_multiply_fusion.6
  50.9 0.1 mul.371
  51.0 0.8 broadcast_multiply_fusion.5
  51.7 0.1 mul.375
  51.8 0.7 convert_element_type.16
  52.6 0.8 broadcast_multiply_fusion.4
  53.3 0.1 mul.379
  53.4 0.8 broadcast_multiply_fusion.3
  54.2 0.1 mul.383
  54.3 0.9 broadcast_multiply_fusion.1
  55.2 0.2 dynamic-slice_reduce_fusion
  55.4 0.1 broadcast_in_dim.71
  55.5 0.1 mul.427
  55.6 0.7 reshape.344
  56.2 2.6 broadcast_multiply_fusion
  58.8 6.3 %fusion.2 = f32[64,64,256]{2,0,1:T(8,128)S(1)} fusion(f32[64,64,1]{1,0,2:T(8,128)S(1)} %reshape.344, f32[64,64,256]{2,1,0:T(8,128)S(1)} %bitcast.55), kind=kOutput, calls=%fused_computation.7 | convolution fusion | flops 805306368 | bytes 8404992 | tf_op jit(solution)/shard_map/ab,bcp->acp/dot_general | solution.py:44
  65.1 7.0 %fusion = f32[64,256,64]{1,2,0:T(8,128)} fusion(f32[64,64,1]{1,0,2:T(8,128)S(1)} %reshape.344, f32[64,64,256]{2,0,1:T(8,128)S(1)} %fusion.2), kind=kOutput, calls=%fused_computation.5 | convolution fusion | flops 805306368 | bytes 8404992 | tf_op jit(solution)/shard_map/cd,adp->acp/dot_general | solution.py:45
  72.1 0.0 copy-start.1
  72.1 3.8 gather_fusion
  75.9 1.0 select_multiply_fusion
  76.9 0.0 reduce-scatter.2.cloned.1.call-update
  76.9 0.0 all-reduce.5.cloned.1.call-start
  77.0 0.0 copy-done.1
  77.0 0.1 fusion.19
  77.1 0.2 select_reduce_fusion.2
  77.3 135.4 %reduce-scatter.2.cloned.1.call-done = f32[16,256]{1,0:T(8,128)} async-done(((f32[512,256]{1,0:T(8,128)}), f32[16,256]{1,0:T(8,128)}) %reduce-scatter.2.cloned.1.call-update) | async-done | bytes 16400 | tf_op jit(solution)/shard_map/reduce_scatter | solution.py:52
  212.7 0.8 fusion.14
  213.6 8.9 %all_to_all.5 = f32[8,2,256]{2,1,0:T(2,128)S(1)} all-to-all(f32[8,2,256]{2,1,0:T(2,128)S(1)} %copy.33), channel_id=1, replica_groups=mesh['hi'=4,'lo'=8] {'lo'}, dimensions={0} | all-to-all | bytes 32768 | tf_op jit(solution)/shard_map/all_to_all | solution.py:63
  222.6 1.1 convolution_bitcast_fusion
  223.7 0.0 all-reduce.5.cloned.1.call-update
  223.7 0.0 all-reduce.7.cloned.1.call-start
  223.7 67.5 %all-reduce.5.cloned.1.call-done = f32[256,256]{0,1:T(8,128)} async-done(((f32[256,256]{0,1:T(8,128)}), f32[256,256]{0,1:T(8,128)}) %all-reduce.5.cloned.1.call-update) | async-done | bytes 262160 | tf_op jit(solution)/shard_map/psum | solution.py:13
  291.2 0.0 all-reduce.7.cloned.1.call-update
  291.3 33.8 %all-reduce.7.cloned.1.call-done = f32[256,256]{0,1:T(8,128)} async-done(((f32[256,256]{0,1:T(8,128)}), f32[256,256]{0,1:T(8,128)}) %all-reduce.7.cloned.1.call-update) | async-done | bytes 262160 | tf_op jit(solution)/shard_map/psum | solution.py:13
  325.1 1.0 broadcast_multiply_fusion.2
  326.0 0.1 copy.37
  326.2 1.0 fusion.6
  327.2 11.7 %cholesky.50 = f32[128,128]{1,0:T(8,128)S(1)} custom-call(f32[128,128]{1,0:T(8,128)S(1)} %cholesky.118), custom_call_target="Cholesky" | custom-call | tf_op jit(solution)/shard_map/jit(cholesky)/cholesky | solution.py:68
  338.9 9.8 %custom-call.14 = f32[1,128,128]{1,2,0:T(8,128)S(1)} custom-call(f32[1,128,128]{2,1,0:T(8,128)S(1)} %get-tuple-element.38), custom_call_target="InvertDiagBlocksLowerTriangular" | custom-call | tf_op jit(solution)/shard_map/jit(cholesky)/cholesky | solution.py:68
  348.8 0.2 constant_dynamic-update-slice_fusion.1
  349.0 0.3 convolution_subtract_fusion.1
  349.3 11.7 %cholesky.105 = f32[128,128]{1,0:T(8,128)S(1)} custom-call(f32[128,128]{1,0:T(8,128)S(1)} %convolution_subtract_fusion.1), custom_call_target="Cholesky" | custom-call | tf_op jit(solution)/shard_map/jit(cholesky)/cholesky | solution.py:68
  361.0 0.6 compare_reduce_fusion
  363.0 0.8 copy.38
  363.8 0.1 triangular_solve.44
  363.9 4.1 while.1
  363.9 0.6 fusion.32
  364.5 1.4 bitcast_dynamic-update-slice_fusion.2
  366.0 0.6 fusion.32
  366.6 1.4 bitcast_dynamic-update-slice_fusion.2
  368.0 19.7 %custom-call.15 = f32[2,128,128]{1,2,0:T(8,128)S(1)} custom-call(f32[2,128,128]{2,1,0:T(8,128)S(1)} %get-tuple-element.10), custom_call_target="InvertDiagBlocksLowerTriangular" | custom-call | tf_op jit(solution)/shard_map/triangular_solve | solution.py:69
  387.7 0.0 copy-start
  387.7 3.7 fusion.4
  391.4 0.0 copy-done
  391.4 3.4 convolution_subtract_fusion
  394.8 2.0 fusion.9
  396.9 2.4 pad_maximum_fusion
  399.3 5.6 %copy.39 = f32[4096,256]{1,0:T(8,128)} copy(f32[4096,256]{0,1:T(8,128)} %pad_maximum_fusion) | data formatting | bytes 8388608
  404.9 0.6 copy.63
  (17 shorter events, 0.2 us)
Async XLA Ops:
  7.2 205.6 %reduce-scatter.2.cloned.1.call-start = ((), (), s32[]{:S(2)}) async-start(), calls=%async_computation.2 | async-start | bytes 540672 | tf_op jit(solution)/shard_map/reduce_scatter | solution.py:52
  72.1 4.9 %copy-start.1 = (s32[16,1]{0,1:T(1,128)S(1)}, s32[16,1]{0,1:T(1,128)}, u32[]{:S(2)}) copy-start(s32[16,1]{0,1:T(1,128)} %param.10) | copy-start | bytes 196
  76.9 214.3 %all-reduce.5.cloned.1.call-start = ((), (), s32[]{:S(2)}) async-start(), calls=%async_computation.3 | async-start | bytes 524288 | tf_op jit(solution)/shard_map/psum | solution.py:13
  223.7 101.4 %all-reduce.7.cloned.1.call-start = ((), (), s32[]{:S(2)}) async-start(), calls=%async_computation.4 | async-start | bytes 524288 | tf_op jit(solution)/shard_map/psum | solution.py:13
  387.7 3.7 copy-start
Sparse Core Ops, SparseCore 0:
  77.1 135.6 reduce-scatter.1
  223.8 67.3 all-reduce.4
  293.6 31.4 all-reduce.6
